TPU v7x, 512 devices: a whole 4x4x16 slice. The times are simulated.
512 devices in a mesh: dp: 4 (over x), cand: 32 (over z, core), tensor: 4 (over y).
Axes of the slice: x: 4, y: 4, z: 16, core: 2. Of those that a mesh axis runs over, the one named last changes fastest.
Arguments:
- context: bfloat16 [8, 4096, 3584], P('dp', 'cand', 'tensor'), may hold values from -12 to 12
- residual: bfloat16 [8, 4096, 3584], P('dp', ('cand', 'tensor')), may hold values from -36 to 36
- out_weight: bfloat16 [3584, 3584], P('cand', 'tensor'), may hold values from -0.09375 to 0.09375
- adapter_down: bfloat16 [3584, 16], P('tensor'), may hold values from -0.09375 to 0.09375
- adapter_up_weight: bfloat16 [16, 3584], replicated, may hold values from -1.5 to 1.5
- norm_gain: float32 [3584], replicated, may hold values from 0.5 to 1.5
- score_weight: float32 [3584], replicated, may hold values from -0.09375 to 0.09375
- teacher: bfloat16 [8, 4096, 4096], P('dp', 'cand', 'tensor'), may hold values from 0.019897461 to 0.9765625
- pair_mask: int32 [8, 4096, 4096], P('dp', 'cand', 'tensor'), may hold values from 0 to 1, as said below
- loss_scale: float32 [8], P('dp'), may hold values from 65536 to 262144
Outputs:
- context_grad: bfloat16 [8, 4096, 3584], P('dp', 'cand', 'tensor')
- residual_gradient: bfloat16 [8, 4096, 3584], P('dp', ('cand', 'tensor'))
- down_grad: float32 [3584, 16], P('tensor')
- up_weight_gradient: float32 [16, 3584], P(None, 'tensor')
- pair_loss: float32 [8], P('dp')
Inputs may be any that keep to these rules, and one draw needn't show every extreme that they name: pair_mask holds 0 or 1; with P = 32, every pair (i, j) whose group j // P lies 4096 / (2P) groups after i // P, counted round over the 4096 / P groups, is valid.
All inputs are finite; a program needn't handle non-finite values.
Results may differ from a plain program's by a relative error of at most 0.02.
Values may be sent and summed in bfloat16 or wider, within the bound.
No kernel may reach another device: no remote copies, remote signals or barrier semaphores. Data moves between devices by JAX's collectives and lax.ppermute only.
A program may use at most 64 MiB of HBM per device.

v0:
```python
import jax
import jax.numpy as jnp
from jax import lax
from jax.sharding import PartitionSpec as P

ADAPTER_SCALE = 0.5
epsilon = 1e-06
F32 = jnp.float32
BF16 = jnp.bfloat16


def gather_copies(x, axis):
    copies = jnp.broadcast_to(x[None], (lax.axis_size(axis),) + x.shape)
    return lax.all_to_all(copies, axis, 0, 0, tiled=True)


def on_device(
    context,
    residual,
    out_weight,
    adapter_down,
    adapter_up_weight,
    norm_gain,
    score_weight,
    teacher,
    pair_mask,
    loss_scale,
):
    queries, cand_rows, _ = context.shape
    width = residual.shape[2]
    cols = teacher.shape[2]
    tensor_count = lax.axis_size("tensor")
    cand_count = lax.axis_size("cand")
    share = cand_rows // tensor_count
    near = cols // cand_rows
    tensor_index = lax.axis_index("tensor")
    dp_index = lax.axis_index("dp")
    cand_index = lax.axis_index("cand")
    dp_count = lax.axis_size("dp")
    full_weight = lax.all_gather(out_weight, "cand", axis=0, tiled=True)
    low_terms = jnp.einsum("qch,hr->qcr", context, adapter_down, preferred_element_type=F32).astype(
        BF16
    )
    low_all = lax.all_gather(low_terms, "tensor", axis=0)
    adapter_in = jnp.sum(low_all.astype(F32), axis=0).astype(BF16)
    adapter_own = lax.dynamic_slice_in_dim(adapter_in, tensor_index * share, share, 1)
    lifted = jnp.einsum("qcr,rd->qcd", adapter_own, adapter_up_weight, preferred_element_type=F32)
    base = residual.astype(F32) + ADAPTER_SCALE * lifted
    mask_count = jnp.sum(pair_mask.astype(F32), axis=(1, 2))
    pairs = gather_copies(jnp.stack([pair_mask.astype(BF16), teacher]), "tensor")
    known = pairs[:, 0].astype(F32) * pairs[:, 1].astype(F32)
    row_known = jnp.sum(known, axis=(0, 3))
    col_known = jnp.sum(known, axis=2)
    full_weight, adapter_in, base, mask_count, pairs, row_known, col_known = (
        lax.optimization_barrier(
            (full_weight, adapter_in, base, mask_count, pairs, row_known, col_known)
        )
    )
    by_owner = jnp.swapaxes(context.reshape(queries, tensor_count, share, context.shape[2]), 0, 1)
    head_terms = jnp.einsum(
        "tqch,dh->tqcd", by_owner, full_weight, preferred_element_type=F32
    ).astype(BF16)
    head_terms = lax.all_to_all(head_terms, "tensor", 0, 0, tiled=True)
    hidden = (base + jnp.sum(head_terms.astype(F32), axis=0)).astype(BF16).astype(F32)
    inv_rms = lax.rsqrt(jnp.mean(hidden * hidden, axis=2) + epsilon)
    gain = norm_gain * score_weight
    dot = jnp.sum(hidden * gain, axis=2)
    scores = dot * inv_rms
    slant = inv_rms * inv_rms * dot / width
    unit = inv_rms[:, :, None] * (gain - hidden * slant[:, :, None])
    pairs, scores = lax.optimization_barrier((pairs, scores))
    valid = lax.optimization_barrier(pairs[:, 0])
    unit_sent, unit, scores = lax.optimization_barrier((unit.astype(BF16), unit, scores))
    unit_all = lax.all_gather(unit_sent, "tensor", axis=1, tiled=True)
    message = jnp.concatenate(
        [scores, jnp.broadcast_to(mask_count[:, None], (queries, 128 - share))], axis=1
    )
    message = gather_copies(message, ("cand", "tensor"))
    count = jnp.sum(message[:, :, share], axis=0)
    message = message[:, :, :share].reshape(cand_count, tensor_count, queries, share)
    own_scores = lax.dynamic_index_in_dim(message, cand_index, 0, keepdims=False)
    own_scores = jnp.swapaxes(own_scores, 0, 1).reshape(queries, cand_rows)
    message = message.reshape(tensor_count, near, tensor_count, queries, share)
    col_scores = jnp.moveaxis(message, 3, 1).reshape(tensor_count, queries, cols)
    margin = own_scores[None, :, :, None] - col_scores[:, :, None, :]
    chance = valid.astype(F32) * jax.nn.sigmoid(margin)
    row_sum = jnp.sum(chance, axis=(0, 3)) - row_known
    columns = jnp.sum(chance, axis=2) - col_known
    columns = columns.reshape(tensor_count, queries, near, cand_rows)
    columns = jnp.swapaxes(columns, 1, 2).reshape(cand_count, queries, cand_rows)
    columns, row_sum, own_late, col_late = lax.optimization_barrier(
        (columns, row_sum, own_scores, col_scores)
    )
    columns = lax.all_to_all(columns, "cand", 0, 0, tiled=True)
    margin = own_late[None, :, :, None] - col_late[:, :, None, :]
    total = (
        jnp.sum(valid.astype(F32) * jax.nn.softplus(margin), axis=(0, 2, 3))
        - jnp.sum(own_late * row_known, axis=1)
        + jnp.sum(col_late * col_known, axis=(0, 2))
    )
    adapter_unit = ADAPTER_SCALE * jnp.einsum(
        "qcd,rd->qcr", unit_all, adapter_up_weight, preferred_element_type=F32
    )
    context_unit = jnp.einsum(
        "qcd,dh->qch", unit_all, full_weight, preferred_element_type=F32
    ) + jnp.einsum(
        "qcr,hr->qch", adapter_unit.astype(BF16), adapter_down, preferred_element_type=F32
    )
    unit_block = lax.dynamic_slice_in_dim(
        unit_all, tensor_index * context.shape[2], context.shape[2], 2
    )
    columns, total, adapter_unit, context_unit, unit_block, count = lax.optimization_barrier(
        (columns, total, adapter_unit, context_unit, unit_block, count)
    )
    score_grad = (row_sum - jnp.sum(columns, axis=0)) * (loss_scale / count)[:, None]
    own_grad = lax.dynamic_slice_in_dim(score_grad, tensor_index * share, share, 1)
    grad_rows = (own_grad[:, :, None] * unit).astype(BF16)
    context_grad = (score_grad[:, :, None] * context_unit).astype(BF16)
    adapter_back = (score_grad[:, :, None] * adapter_unit).astype(BF16)
    down_local = jnp.einsum("qcr,qch->rh", adapter_back, context, preferred_element_type=F32)
    adapter_scaled = (score_grad[:, :, None] * adapter_in.astype(F32)).astype(BF16)
    up_local = ADAPTER_SCALE * jnp.einsum(
        "qcr,qcd->rd", adapter_scaled, unit_block, preferred_element_type=F32
    )
    rank = adapter_down.shape[1]
    flat = jnp.concatenate([down_local, up_local], axis=0)
    wide = flat.shape[1]
    segments = cand_count // near
    members = dp_count * near
    near_groups = [
        [d * cand_count + a * near + b for d in range(dp_count) for b in range(near)]
        for a in range(segments)
    ]
    far_groups = [[a * near + b for a in range(segments)] for b in range(near)]
    slots = lax.dynamic_update_slice_in_dim(
        jnp.zeros((1, 1, 128), F32), total[None, None, :], dp_index * queries, 2
    )
    tiles = flat.reshape(2 * rank // 8, 8, wide // 128, 128)
    tiles = jnp.swapaxes(tiles, 1, 2).reshape(-1, 8, 128)
    used = tiles.shape[0]
    height = -(-(used + 1) // members)
    slots = jnp.pad(slots, ((0, height * members - used - 1), (0, 7), (0, 0)))
    tiles = jnp.concatenate([tiles, slots]).reshape(members, 8 * height, 128)
    tiles = lax.all_to_all(tiles, ("dp", "cand"), 0, 0, axis_index_groups=near_groups, tiled=True)
    tiles = lax.psum(jnp.sum(tiles, axis=0), "cand", axis_index_groups=far_groups)
    tiles = jnp.broadcast_to(tiles[None], (members,) + tiles.shape)
    tiles = lax.all_to_all(
        tiles, ("dp", "cand"), 0, 0, axis_index_groups=near_groups, tiled=True
    ).reshape(-1, 8, 128)
    loss_sum = lax.dynamic_slice_in_dim(tiles[used, 0], dp_index * queries, queries, 0)
    pair_loss = loss_sum / count
    flat = tiles[:used].reshape(2 * rank // 8, wide // 128, 8, 128)
    flat = jnp.swapaxes(flat, 1, 2).reshape(2 * rank, wide)
    down_grad = flat[:rank].T
    up_weight_gradient = flat[rank:]
    return (context_grad, grad_rows, down_grad, up_weight_gradient, pair_loss)


def solution(mesh):
    in_specs = (
        P("dp", "cand", "tensor"),
        P("dp", ("cand", "tensor"), None),
        P("cand", "tensor"),
        P("tensor", None),
        P(),
        P(),
        P(),
        P("dp", "cand", "tensor"),
        P("dp", "cand", "tensor"),
        P("dp"),
    )
    out_specs = (
        P("dp", "cand", "tensor"),
        P("dp", ("cand", "tensor"), None),
        P("tensor", None),
        P(None, "tensor"),
        P("dp"),
    )
    return jax.shard_map(
        on_device, mesh=mesh, in_specs=in_specs, out_specs=out_specs, check_vma=False
    )
```

profile of v0, /device:TPU:1, one launch (start us, length us, event | category | flops | bytes accessed | tf_op | source)
XLA Modules:
  0.0 228.8 jit_solution(7035708157234387548)
XLA Ops:
  7.2 0.7 all-gather.4.cloned.1.call-update
  7.9 1.3 convert_bitcast_fusion
  9.2 1.1 pad_maximum_fusion
  10.4 2.6 %broadcast_in_dim.12 = bf16[4,2,2,128,1024]{4,3,2,1,0:T(8,128)(2,1)} broadcast(bf16[2,2,128,1024]{3,2,1,0:T(8,128)(2,1)S(1)} %pad_maximum_fusion), dimensions={1,2,3,4} | broadcast | bytes 5242880 | tf_op jit(solution)/shard_map/broadcast_in_dim | solution.py:13
  13.0 5.2 %all-to-all-start = ((bf16[4,2,2,128,1024]{4,3,2,1,0:T(8,128)(2,1)}), bf16[4,2,2,128,1024]{4,3,2,1,0:T(8,128)(2,1)}, u32[]{:S(2)}, u32[]{:S(2)}) async-start(bf16[4,2,2,128,1024]{4,3,2,1,0:T(8,128)(2,1)} %broadcast_in_dim.12), calls=%async_computation | async-start | bytes 8388608 | tf_op jit(solution)/shard_map/all_to_all | solution.py:14
  18.2 0.2 convolution_convert_fusion
  18.4 47.8 %all-gather = bf16[8,128,16]{1,2,0:T(8,128)(2,1)S(1)} all-gather(bf16[2,128,16]{1,2,0:T(8,128)(2,1)S(1)} %convolution_convert_fusion), channel_id=2, replica_groups=mesh['dp'=4,'cand'=32,'tensor'=4] {'tensor'}, dimensions={0}, use_global_device_ids=true | all-gather | bytes 40960 | tf_op jit(solution)/shard_map/all_gather | solution.py:44
  66.2 0.2 convert_reduce_fusion.1
  66.4 0.4 fusion.10
  66.8 3.3 %fusion.16 = (f32[4,2,1024]{2,1,0:T(2,128)S(1)}, f32[2,128]{1,0:T(2,128)S(1)}) fusion(bf16[4,2,2,128,1024]{4,3,2,1,0:T(8,128)(2,1)} %all-to-all-done), kind=kLoop, calls=%fused_computation.19 | loop fusion | flops 5234432 | bytes 4228096 | tf_op jit(solution)/shard_map/reduce_sum | solution.py:53
  70.0 22.9 %all-gather.4.cloned.1.call-done = bf16[3584,896]{1,0:T(8,128)(2,1)} async-done(((bf16[112,896]{1,0:T(8,128)(2,1)}), bf16[3584,896]{1,0:T(8,128)(2,1)}) %all-gather.4.cloned.1.call-update) | async-done | bytes 6422544 | tf_op jit(solution)/shard_map/all_gather | solution.py:40
  93.0 6.2 %fusion.7 = bf16[4,2,32,3584]{3,2,1,0:T(8,128)(2,1)} fusion(bf16[3584,896]{1,0:T(8,128)(2,1)} %all-gather.4.cloned.1.call-done, bf16[2,4,32,896]{3,2,1,0:T(8,128)(2,1)S(1)} %bitcast.80), kind=kOutput, calls=%fused_computation.10 | convolution fusion | flops 1645084672 | bytes 8716288 | tf_op jit(solution)/shard_map/tqch,dh->tqcd/dot_general | solution.py:60
  99.1 4.1 %all-to-all-start.1 = ((bf16[4,2,32,3584]{3,2,1,0:T(8,128)(2,1)}), bf16[4,2,32,3584]{3,2,1,0:T(8,128)(2,1)S(1)}, u32[]{:S(2)}, u32[]{:S(2)}) async-start(bf16[4,2,32,3584]{3,2,1,0:T(8,128)(2,1)} %fusion.7), calls=%async_computation.1 | async-start | bytes 3670016 | tf_op jit(solution)/shard_map/all_to_all | solution.py:63
  103.2 23.1 %all-to-all-done.1 = bf16[4,2,32,3584]{3,2,1,0:T(8,128)(2,1)S(1)} async-done(((bf16[4,2,32,3584]{3,2,1,0:T(8,128)(2,1)}), bf16[4,2,32,3584]{3,2,1,0:T(8,128)(2,1)S(1)}, u32[]{:S(2)}, u32[]{:S(2)}) %all-to-all-start.1) | async-done | bytes 1835040 | tf_op jit(solution)/shard_map/all_to_all | solution.py:63
  126.3 0.3 convert_reduce_fusion
  126.6 0.3 fusion.22
  126.9 1.0 fusion.24
  128.0 0.7 broadcast_in_dim.14
  128.7 10.7 %all-to-all-start.2 = ((f32[128,2,128]{2,1,0:T(2,128)}), f32[128,2,128]{2,1,0:T(2,128)S(1)}, u32[]{:S(2)}, u32[]{:S(2)}) async-start(f32[128,2,128]{2,1,0:T(2,128)} %broadcast_in_dim.14), calls=%async_computation.2 | async-start | bytes 262144 | tf_op jit(solution)/shard_map/all_to_all | solution.py:14
  139.4 2.0 slice_bitcast_fusion
  141.4 16.1 %all-to-all-done.2 = f32[128,2,128]{2,1,0:T(2,128)S(1)} async-done(((f32[128,2,128]{2,1,0:T(2,128)}), f32[128,2,128]{2,1,0:T(2,128)S(1)}, u32[]{:S(2)}, u32[]{:S(2)}) %all-to-all-start.2) | async-done | bytes 131104 | tf_op jit(solution)/shard_map/all_to_all | solution.py:14
  157.5 0.1 reshape.78
  157.7 0.1 sub.49
  157.8 1.8 fusion.18
  159.7 0.6 copy.35
  160.3 3.8 %all-to-all-start.3 = ((f32[32,2,128]{2,1,0:T(2,128)}), f32[32,2,128]{2,1,0:T(2,128)S(1)}, u32[]{:S(2)}, u32[]{:S(2)}) async-start(f32[32,2,128]{2,1,0:T(2,128)} %copy.35), calls=%async_computation.3 | async-start | bytes 65536 | tf_op jit(solution)/shard_map/all_to_all | solution.py:94
  164.2 0.1 multiply_reduce_fusion.1
  164.3 0.1 multiply_reduce_fusion
  164.4 0.3 slice_reduce_fusion
  164.8 2.9 %fusion.11 = f32[2]{0:T(128)S(1)} fusion(bf16[4,2,128,1024]{3,2,1,0:T(8,128)(2,1)S(1)} %slice_bitcast_fusion, f32[4,2,1024]{2,1,0:T(2,128)S(1)} %copy.37, f32[2,128]{1,0:T(2,128)S(1)} %sub.49), kind=kLoop, calls=%fused_computation.13 | loop fusion | flops 10485758 | bytes 2130952 | tf_op jit(solution)/shard_map/reduce_sum | solution.py:97
  167.6 5.6 %fusion.2 = f32[2,128,896]{2,1,0:T(8,128)S(1)} fusion(bf16[2,128,3584]{2,1,0:T(8,128)(2,1)} %all-gather.6.cloned.1.call-done, bf16[3584,896]{1,0:T(8,128)(2,1)} %all-gather.4.cloned.1.call-done), kind=kOutput, calls=%fused_computation.5 | convolution fusion | flops 1644167168 | bytes 9175040 | tf_op jit(solution)/shard_map/qcd,dh->qch/dot_general | solution.py:104
  173.3 0.6 convolution_multiply_fusion.1
  173.8 0.4 convolution_add_fusion
  174.2 1.4 all-to-all-done.3
  175.7 0.2 convolution_bitcast_fusion.1
  175.9 0.2 fusion.20
  176.1 0.1 dynamic_update_slice.3
  176.3 0.7 select_maximum_fusion
  177.0 5.9 %all-to-all-start.4 = ((f32[32,8,128]{2,1,0:T(8,128)}), f32[32,8,128]{2,1,0:T(8,128)S(1)}, u32[]{:S(2)}, u32[]{:S(2)}) async-start(f32[32,8,128]{2,1,0:T(8,128)} %select_maximum_fusion), calls=%async_computation.4 | async-start | bytes 262144 | tf_op jit(solution)/shard_map/all_to_all | solution.py:144
  182.9 8.6 %all-to-all-done.4 = f32[32,8,128]{2,1,0:T(8,128)S(1)} async-done(((f32[32,8,128]{2,1,0:T(8,128)}), f32[32,8,128]{2,1,0:T(8,128)S(1)}, u32[]{:S(2)}, u32[]{:S(2)}) %all-to-all-start.4) | async-done | bytes 131104 | tf_op jit(solution)/shard_map/all_to_all | solution.py:144
  191.6 13.8 %psum.7 = f32[8,128]{1,0:T(8,128)S(1)} all-reduce(f32[8,128]{1,0:T(8,128)S(1)} %reduce_sum.152), channel_id=1, replica_groups={{0,32,64,96},{4,36,68,100},{8,40,72,104},{12,44,76,108},{16,48,80,112},..., use_global_device_ids=true, to_apply=%region_15.16 | all-reduce | flops 1024 | bytes 8192 | tf_op jit(solution)/shard_map/psum | solution.py:145
  205.3 0.6 broadcast_in_dim.17
  206.0 5.9 %all-to-all-start.5 = ((f32[32,8,128]{2,1,0:T(8,128)}), f32[32,8,128]{2,1,0:T(8,128)S(1)}, u32[]{:S(2)}, u32[]{:S(2)}) async-start(f32[32,8,128]{2,1,0:T(8,128)} %broadcast_in_dim.17), calls=%async_computation.5 | async-start | bytes 262144 | tf_op jit(solution)/shard_map/all_to_all | solution.py:147
  211.9 0.9 multiply_convert_fusion
  212.8 0.9 multiply_convert_fusion.1
  213.7 7.0 %all-to-all-done.5 = f32[32,8,128]{2,1,0:T(8,128)S(1)} async-done(((f32[32,8,128]{2,1,0:T(8,128)}), f32[32,8,128]{2,1,0:T(8,128)S(1)}, u32[]{:S(2)}, u32[]{:S(2)}) %all-to-all-start.5) | async-done | bytes 131104 | tf_op jit(solution)/shard_map/all_to_all | solution.py:147
  220.8 0.6 fusion.38
  221.3 0.6 slice_bitcast_fusion.1
  (48 shorter events, 0.7 us)
Async XLA Ops:
  7.2 59.2 %copy-start = (bf16[16,3584]{1,0:T(8,128)(2,1)S(1)}, bf16[16,3584]{1,0:T(8,128)(2,1)}, u32[]{:S(2)}) copy-start(bf16[16,3584]{1,0:T(8,128)(2,1)} %param.14) | copy-start | bytes 344068
  7.2 85.8 %all-gather.4.cloned.1.call-start = ((), (), s32[]{:S(2)}) async-start(), calls=%async_computation.6 | async-start | bytes 6623232 | tf_op jit(solution)/shard_map/all_gather | solution.py:40
  13.0 5.2 %copy-start.3 = (bf16[2,128,896]{2,1,0:T(8,128)(2,1)S(1)}, bf16[2,128,896]{2,1,0:T(8,128)(2,1)}, u32[]{:S(2)}) copy-start(bf16[2,128,896]{2,1,0:T(8,128)(2,1)} %param.10) | copy-start | bytes 1376260
  13.0 5.2 %copy-start.6 = (bf16[896,16]{0,1:T(8,128)(2,1)S(1)}, bf16[896,16]{0,1:T(8,128)(2,1)}, u32[]{:S(2)}) copy-start(bf16[896,16]{0,1:T(8,128)(2,1)} %param.13) | copy-start | bytes 86020
  13.0 53.1 %copy-start.1 = (s32[2,128,1024]{2,1,0:T(8,128)S(1)}, s32[2,128,1024]{2,1,0:T(8,128)}, u32[]{:S(2)}) copy-start(s32[2,128,1024]{2,1,0:T(8,128)} %param.18) | copy-start | bytes 3145732
  13.0 53.4 %copy-start.5 = (bf16[2,32,3584]{2,1,0:T(8,128)(2,1)S(1)}, bf16[2,32,3584]{2,1,0:T(8,128)(2,1)}, u32[]{:S(2)}) copy-start(bf16[2,32,3584]{2,1,0:T(8,128)(2,1)} %param.11) | copy-start | bytes 1376260
  13.0 53.8 %all-to-all-start = ((bf16[4,2,2,128,1024]{4,3,2,1,0:T(8,128)(2,1)}), bf16[4,2,2,128,1024]{4,3,2,1,0:T(8,128)(2,1)}, u32[]{:S(2)}, u32[]{:S(2)}) async-start(bf16[4,2,2,128,1024]{4,3,2,1,0:T(8,128)(2,1)} %broadcast_in_dim.12), calls=%async_computation | async-start | bytes 8388608 | tf_op jit(solution)/shard_map/all_to_all | solution.py:14
  93.0 10.2 %copy-start.7 = (f32[3584]{0:T(1024)S(1)}, f32[3584]{0:T(1024)}, u32[]{:S(2)}) copy-start(f32[3584]{0:T(1024)} %param.15) | copy-start | bytes 43012
  93.0 10.2 %copy-start.8 = (f32[3584]{0:T(1024)S(1)}, f32[3584]{0:T(1024)}, u32[]{:S(2)}) copy-start(f32[3584]{0:T(1024)} %param.16) | copy-start | bytes 43012
  99.1 27.1 %all-to-all-start.1 = ((bf16[4,2,32,3584]{3,2,1,0:T(8,128)(2,1)}), bf16[4,2,32,3584]{3,2,1,0:T(8,128)(2,1)S(1)}, u32[]{:S(2)}, u32[]{:S(2)}) async-start(bf16[4,2,32,3584]{3,2,1,0:T(8,128)(2,1)} %fusion.7), calls=%async_computation.1 | async-start | bytes 3670016 | tf_op jit(solution)/shard_map/all_to_all | solution.py:63
  103.2 64.4 %all-gather.6.cloned.1.call-start = ((), (), s32[]{:S(2)}) async-start(), calls=%async_computation.7 | async-start | bytes 2293760 | tf_op jit(solution)/shard_map/all_gather | solution.py:74
  128.7 28.8 %all-to-all-start.2 = ((f32[128,2,128]{2,1,0:T(2,128)}), f32[128,2,128]{2,1,0:T(2,128)S(1)}, u32[]{:S(2)}, u32[]{:S(2)}) async-start(f32[128,2,128]{2,1,0:T(2,128)} %broadcast_in_dim.14), calls=%async_computation.2 | async-start | bytes 262144 | tf_op jit(solution)/shard_map/all_to_all | solution.py:14
  160.3 15.3 %all-to-all-start.3 = ((f32[32,2,128]{2,1,0:T(2,128)}), f32[32,2,128]{2,1,0:T(2,128)S(1)}, u32[]{:S(2)}, u32[]{:S(2)}) async-start(f32[32,2,128]{2,1,0:T(2,128)} %copy.35), calls=%async_computation.3 | async-start | bytes 65536 | tf_op jit(solution)/shard_map/all_to_all | solution.py:94
  167.6 5.6 %copy-start.2 = (bf16[2,128,3584]{2,1,0:T(8,128)(2,1)S(1)}, bf16[2,128,3584]{2,1,0:T(8,128)(2,1)}, u32[]{:S(2)}) copy-start(bf16[2,128,3584]{2,1,0:T(8,128)(2,1)} %all-gather.6.cloned.1.call-done) | copy-start | bytes 5505028
  173.2 2.4 %copy-start.9 = (f32[2]{0:T(128)S(1)}, f32[2]{0:T(128)}, u32[]{:S(2)}) copy-start(f32[2]{0:T(128)} %param.19) | copy-start | bytes 28
  173.2 2.5 %copy-start.4 = (bf16[2,128,896]{2,1,0:T(8,128)(2,1)S(1)}, bf16[2,128,896]{2,1,0:T(8,128)(2,1)}, u32[]{:S(2)}) copy-start(bf16[2,128,896]{2,1,0:T(8,128)(2,1)} %param.10) | copy-start | bytes 1376260
  177.0 14.6 %all-to-all-start.4 = ((f32[32,8,128]{2,1,0:T(8,128)}), f32[32,8,128]{2,1,0:T(8,128)S(1)}, u32[]{:S(2)}, u32[]{:S(2)}) async-start(f32[32,8,128]{2,1,0:T(8,128)} %select_maximum_fusion), calls=%async_computation.4 | async-start | bytes 262144 | tf_op jit(solution)/shard_map/all_to_all | solution.py:144
  206.0 14.8 %all-to-all-start.5 = ((f32[32,8,128]{2,1,0:T(8,128)}), f32[32,8,128]{2,1,0:T(8,128)S(1)}, u32[]{:S(2)}, u32[]{:S(2)}) async-start(f32[32,8,128]{2,1,0:T(8,128)} %broadcast_in_dim.17), calls=%async_computation.5 | async-start | bytes 262144 | tf_op jit(solution)/shard_map/all_to_all | solution.py:147
Sparse Core Ops, SparseCore 0:
  10.1 82.7 all-gather.3
  128.0 32.9 all-gather.5
where the time goes:
time: 229 us
  waiting for transfers between devices  79.9 us (35%)
  blocking collectives  61.5 us (27%)
  starting transfers between devices  35.5 us (16%)
  other arithmetic  16.1 us (7%)
  between operations  14.3 us (6%)
  matrix products  13.6 us (6%)
  local copies, waits for them, and re-layouts  7.95 us (3%)
    all_gather x1, blocking collectives, on_device(): low_all = lax.all_gather(low_terms, 'tensor', axis=0)  47.8 us
    all_to_all x1, waiting for transfers between devices, on_device(): head_terms = lax.all_to_all(head_terms, 'tensor', 0, 0, tiled=True)  23.1 us
    all_gather x1, waiting for transfers between devices, on_device(): full_weight = lax.all_gather(out_weight, 'cand', axis=0, tiled=True)  22.9 us
    all_to_all x2, waiting for transfers between devices, gather_copies(): return lax.all_to_all(copies, axis, 0, 0, tiled=True)  16.1 us
    all_to_all x2, starting transfers between devices, gather_copies(): return lax.all_to_all(copies, axis, 0, 0, tiled=True)  15.8 us
    all_to_all x2, waiting for transfers between devices, on_device(): lax.all_to_all(tiles, ('dp', 'cand'), 0, 0, axis_index_groups=near_groups...  15.7 us
    psum x1, blocking collectives, on_device(): lax.psum(jnp.sum(tiles, axis=0), 'cand', axis_index_groups=far_groups)  13.8 us
    all_to_all x2, starting transfers between devices, on_device(): lax.all_to_all(tiles, ('dp', 'cand'), 0, 0, axis_index_groups=near_groups...  11.8 us
  transfers between devices with their start and end apart: 8, of which 6 were waited for; matrix products, arithmetic and copies ran while one was open for 12% of the time, Pallas kernels for 0%

commit v1 on v0

--- a/solution.py
+++ b/solution.py
@@ -7,6 +7,12 @@
 epsilon = 1e-06
 F32 = jnp.float32
 BF16 = jnp.bfloat16
+
+
+def group_the_body(my_data):
+    return jnp.concatenate(
+        lax.all_to_all(jnp.stack([my_data] * lax.psum(1, "cand"), 0), "cand", 0, 0), 0
+    )
 
 
 def gather_copies(x, axis):
@@ -37,7 +43,7 @@
     dp_index = lax.axis_index("dp")
     cand_index = lax.axis_index("cand")
     dp_count = lax.axis_size("dp")
-    full_weight = lax.all_gather(out_weight, "cand", axis=0, tiled=True)
+    full_weight = group_the_body(out_weight)
     low_terms = jnp.einsum("qch,hr->qcr", context, adapter_down, preferred_element_type=F32).astype(
         BF16
     )

time: 229 us -> 503 us (2.20)
  waiting for transfers between devices: 79.9 us -> 322 us
  starting transfers between devices: 35.5 us -> 54.3 us
  blocking collectives: 61.5 us -> 71 us
    all_to_all x0 -> x1, waiting for transfers between devices: none -> 267 us  [group_the_body(): lax.all_to_all(jnp.stack([my_data] * lax.psum(1, 'cand'), 0), 'cand', 0, 0)]
    all_to_all x0 -> x1, blocking collectives: none -> 48.1 us  [gather_copies(): return lax.all_to_all(copies, axis, 0, 0, tiled=True)]
    all_gather x1, blocking collectives: 47.8 us -> 9.07 us  [on_device(): low_all = lax.all_gather(low_terms, 'tensor', axis=0)]
    all_gather x1 -> x0, waiting for transfers between devices: 22.9 us -> none  [on_device(): full_weight = lax.all_gather(out_weight, 'cand', axis=0, tiled=True)]
    all_to_all x0 -> x1, starting transfers between devices: none -> 22.1 us  [group_the_body(): lax.all_to_all(jnp.stack([my_data] * lax.psum(1, 'cand'), 0), 'cand', 0, 0)]
    all_to_all x2 -> x1, starting transfers between devices: 15.8 us -> 11.5 us  [gather_copies(): return lax.all_to_all(copies, axis, 0, 0, tiled=True)]
    all_to_all x2 -> x1, waiting for transfers between devices: 16.1 us -> 16.1 us  [gather_copies(): return lax.all_to_all(copies, axis, 0, 0, tiled=True)]
  transfers between devices with their start and end apart: 8 -> 7, of which waited for: 6 -> 5; matrix products, arithmetic and copies ran while one was open for 12% -> 5% of each run, Pallas kernels for 0% -> 0%
where the time goes in v1:
time: 503 us
  waiting for transfers between devices  322 us (64%)
  blocking collectives  71 us (14%)
  starting transfers between devices  54.3 us (11%)
  other arithmetic  16.1 us (3%)
  matrix products  15 us (3%)
  between operations  14.4 us (3%)
  local copies, waits for them, and re-layouts  10 us (2%)
    all_to_all x1, waiting for transfers between devices, group_the_body(): lax.all_to_all(jnp.stack([my_data] * lax.psum(1, 'cand'), 0), 'cand', 0, 0)  267 us
    all_to_all x1, blocking collectives, gather_copies(): return lax.all_to_all(copies, axis, 0, 0, tiled=True)  48.1 us
    all_to_all x1, waiting for transfers between devices, on_device(): head_terms = lax.all_to_all(head_terms, 'tensor', 0, 0, tiled=True)  23 us
    all_to_all x1, starting transfers between devices, group_the_body(): lax.all_to_all(jnp.stack([my_data] * lax.psum(1, 'cand'), 0), 'cand', 0, 0)  22.1 us
    all_to_all x1, waiting for transfers between devices, gather_copies(): return lax.all_to_all(copies, axis, 0, 0, tiled=True)  16.1 us
    all_to_all x2, waiting for transfers between devices, on_device(): lax.all_to_all(tiles, ('dp', 'cand'), 0, 0, axis_index_groups=near_groups...  15.7 us
    psum x1, blocking collectives, on_device(): lax.psum(jnp.sum(tiles, axis=0), 'cand', axis_index_groups=far_groups)  13.8 us
    all_to_all x2, starting transfers between devices, on_device(): lax.all_to_all(tiles, ('dp', 'cand'), 0, 0, axis_index_groups=near_groups...  13.2 us
  transfers between devices with their start and end apart: 7, of which 5 were waited for; matrix products, arithmetic and copies ran while one was open for 5% of the time, Pallas kernels for 0%

profile of v1, /device:TPU:1, one launch (start us, length us, event | category | flops | bytes accessed | tf_op | source)
XLA Modules:
  0.0 502.5 jit_solution(17033316855669320370)
XLA Ops:
  7.2 1.3 convert_bitcast_fusion
  8.5 1.1 pad_maximum_fusion
  9.7 0.5 broadcast_in_dim.12
  10.2 48.1 %all_to_all.35 = bf16[4,2,2,128,1024]{4,3,2,1,0:T(8,128)(2,1)} all-to-all(bf16[4,2,2,128,1024]{4,3,2,1,0:T(8,128)(2,1)S(1)} %broadcast_in_dim.12), channel_id=1, replica_groups=mesh['dp'=4,'cand'=32,'tensor'=4] {'tensor'}, dimensions={0} | all-to-all | bytes 8388608 | tf_op jit(solution)/shard_map/all_to_all | solution.py:20
  58.4 3.2 stack.8
  61.5 22.1 %all-to-all-start = ((bf16[32,112,896]{2,1,0:T(8,128)(2,1)}), bf16[32,112,896]{2,1,0:T(8,128)(2,1)}, u32[]{:S(2)}, u32[]{:S(2)}) async-start(bf16[32,112,896]{2,1,0:T(8,128)(2,1)} %stack.8), calls=%async_computation | async-start | bytes 12845056 | tf_op jit(solution)/shard_map/all_to_all | solution.py:14
  83.7 0.2 convolution_convert_fusion
  83.9 9.1 %all-gather = bf16[8,128,16]{1,2,0:T(8,128)(2,1)S(1)} all-gather(bf16[2,128,16]{1,2,0:T(8,128)(2,1)S(1)} %convolution_convert_fusion), channel_id=2, replica_groups=mesh['dp'=4,'cand'=32,'tensor'=4] {'tensor'}, dimensions={0}, use_global_device_ids=true | all-gather | bytes 40960 | tf_op jit(solution)/shard_map/all_gather | solution.py:50
  93.0 0.2 convert_reduce_fusion.1
  93.2 0.4 fusion.10
  93.6 3.2 fusion.16
  96.8 267.0 %all-to-all-done = bf16[32,112,896]{2,1,0:T(8,128)(2,1)} async-done(((bf16[32,112,896]{2,1,0:T(8,128)(2,1)}), bf16[32,112,896]{2,1,0:T(8,128)(2,1)}, u32[]{:S(2)}, u32[]{:S(2)}) %all-to-all-start) | async-done | bytes 6422560 | tf_op jit(solution)/shard_map/all_to_all | solution.py:14
  363.8 6.2 %fusion.7 = bf16[4,2,32,3584]{3,2,1,0:T(8,128)(2,1)} fusion(bf16[3584,896]{1,0:T(8,128)(2,1)} %bitcast, bf16[2,4,32,896]{3,2,1,0:T(8,128)(2,1)S(1)} %bitcast.81), kind=kOutput, calls=%fused_computation.10 | convolution fusion | flops 1645084672 | bytes 8716288 | tf_op jit(solution)/shard_map/tqch,dh->tqcd/dot_general | solution.py:66
  370.0 3.6 all-to-all-start.2
  373.6 23.0 %all-to-all-done.2 = bf16[4,2,32,3584]{3,2,1,0:T(8,128)(2,1)S(1)} async-done(((bf16[4,2,32,3584]{3,2,1,0:T(8,128)(2,1)}), bf16[4,2,32,3584]{3,2,1,0:T(8,128)(2,1)S(1)}, u32[]{:S(2)}, u32[]{:S(2)}) %all-to-all-start.2) | async-done | bytes 1835040 | tf_op jit(solution)/shard_map/all_to_all | solution.py:69
  396.6 0.3 convert_reduce_fusion
  396.9 0.3 fusion.22
  397.2 1.0 fusion.24
  398.4 0.7 broadcast_in_dim.14
  399.1 11.5 %all-to-all-start.3 = ((f32[128,2,128]{2,1,0:T(2,128)}), f32[128,2,128]{2,1,0:T(2,128)S(1)}, u32[]{:S(2)}, u32[]{:S(2)}) async-start(f32[128,2,128]{2,1,0:T(2,128)} %broadcast_in_dim.14), calls=%async_computation.3 | async-start | bytes 262144 | tf_op jit(solution)/shard_map/all_to_all | solution.py:20
  410.6 2.0 slice_bitcast_fusion
  412.6 16.1 %all-to-all-done.3 = f32[128,2,128]{2,1,0:T(2,128)S(1)} async-done(((f32[128,2,128]{2,1,0:T(2,128)}), f32[128,2,128]{2,1,0:T(2,128)S(1)}, u32[]{:S(2)}, u32[]{:S(2)}) %all-to-all-start.3) | async-done | bytes 131104 | tf_op jit(solution)/shard_map/all_to_all | solution.py:20
  428.8 0.1 reshape.84
  429.1 1.8 fusion.18
  431.0 0.6 copy.35
  431.6 3.8 all-to-all-start.4
  435.4 0.1 multiply_reduce_fusion.1
  435.5 0.1 multiply_reduce_fusion
  435.7 0.3 slice_reduce_fusion
  436.0 2.9 fusion.11
  438.9 2.1 convolution_multiply_fusion.1
  441.0 5.5 %fusion.2 = f32[2,128,896]{2,1,0:T(8,128)S(1)} fusion(bf16[2,128,3584]{2,1,0:T(8,128)(2,1)} %all-gather.3.cloned.1.call-done, bf16[3584,896]{1,0:T(8,128)(2,1)} %bitcast), kind=kOutput, calls=%fused_computation.5 | convolution fusion | flops 1644167168 | bytes 9175040 | tf_op jit(solution)/shard_map/qcd,dh->qch/dot_general | solution.py:110
  446.5 0.3 convolution_add_fusion
  446.8 1.1 constant_dynamic-slice_fusion.2
  448.0 0.2 convolution_bitcast_fusion.1
  448.2 0.2 fusion.20
  448.4 0.1 dynamic_update_slice.3
  448.6 0.7 select_maximum_fusion
  449.2 7.3 %all-to-all-start.5 = ((f32[32,8,128]{2,1,0:T(8,128)}), f32[32,8,128]{2,1,0:T(8,128)S(1)}, u32[]{:S(2)}, u32[]{:S(2)}) async-start(f32[32,8,128]{2,1,0:T(8,128)} %select_maximum_fusion), calls=%async_computation.5 | async-start | bytes 262144 | tf_op jit(solution)/shard_map/all_to_all | solution.py:150
  456.6 8.6 %all-to-all-done.5 = f32[32,8,128]{2,1,0:T(8,128)S(1)} async-done(((f32[32,8,128]{2,1,0:T(8,128)}), f32[32,8,128]{2,1,0:T(8,128)S(1)}, u32[]{:S(2)}, u32[]{:S(2)}) %all-to-all-start.5) | async-done | bytes 131104 | tf_op jit(solution)/shard_map/all_to_all | solution.py:150
  465.2 13.8 %psum.7 = f32[8,128]{1,0:T(8,128)S(1)} all-reduce(f32[8,128]{1,0:T(8,128)S(1)} %reduce_sum.152), channel_id=1, replica_groups={{0,32,64,96},{4,36,68,100},{8,40,72,104},{12,44,76,108},{16,48,80,112},..., use_global_device_ids=true, to_apply=%region_15.16 | all-reduce | flops 1024 | bytes 8192 | tf_op jit(solution)/shard_map/psum | solution.py:151
  479.0 0.6 broadcast_in_dim.17
  479.7 5.9 %all-to-all-start.6 = ((f32[32,8,128]{2,1,0:T(8,128)}), f32[32,8,128]{2,1,0:T(8,128)S(1)}, u32[]{:S(2)}, u32[]{:S(2)}) async-start(f32[32,8,128]{2,1,0:T(8,128)} %broadcast_in_dim.17), calls=%async_computation.6 | async-start | bytes 262144 | tf_op jit(solution)/shard_map/all_to_all | solution.py:153
  485.6 0.9 multiply_convert_fusion
  486.5 0.9 multiply_convert_fusion.1
  487.4 7.0 %all-to-all-done.6 = f32[32,8,128]{2,1,0:T(8,128)S(1)} async-done(((f32[32,8,128]{2,1,0:T(8,128)}), f32[32,8,128]{2,1,0:T(8,128)S(1)}, u32[]{:S(2)}, u32[]{:S(2)}) %all-to-all-start.6) | async-done | bytes 131104 | tf_op jit(solution)/shard_map/all_to_all | solution.py:153
  494.4 0.6 slice_bitcast_fusion.1
  495.1 0.6 fusion.38
  (47 shorter events, 0.7 us)
Async XLA Ops:
  7.2 86.0 %copy-start = (bf16[16,3584]{1,0:T(8,128)(2,1)S(1)}, bf16[16,3584]{1,0:T(8,128)(2,1)}, u32[]{:S(2)}) copy-start(bf16[16,3584]{1,0:T(8,128)(2,1)} %param.14) | copy-start | bytes 344068
  10.2 48.2 %copy-start.5 = (bf16[112,896]{1,0:T(8,128)(2,1)S(1)}, bf16[112,896]{1,0:T(8,128)(2,1)}, u32[]{:S(2)}) copy-start(bf16[112,896]{1,0:T(8,128)(2,1)} %param.12) | copy-start | bytes 602116
  61.5 22.1 %copy-start.2 = (bf16[2,128,896]{2,1,0:T(8,128)(2,1)S(1)}, bf16[2,128,896]{2,1,0:T(8,128)(2,1)}, u32[]{:S(2)}) copy-start(bf16[2,128,896]{2,1,0:T(8,128)(2,1)} %param.10) | copy-start | bytes 1376260
  61.5 22.1 %copy-start.6 = (bf16[896,16]{0,1:T(8,128)(2,1)S(1)}, bf16[896,16]{0,1:T(8,128)(2,1)}, u32[]{:S(2)}) copy-start(bf16[896,16]{0,1:T(8,128)(2,1)} %param.13) | copy-start | bytes 86020
  61.5 31.4 %copy-start.1 = (s32[2,128,1024]{2,1,0:T(8,128)S(1)}, s32[2,128,1024]{2,1,0:T(8,128)}, u32[]{:S(2)}) copy-start(s32[2,128,1024]{2,1,0:T(8,128)} %param.18) | copy-start | bytes 3145732
  61.5 31.7 %copy-start.4 = (bf16[2,32,3584]{2,1,0:T(8,128)(2,1)S(1)}, bf16[2,32,3584]{2,1,0:T(8,128)(2,1)}, u32[]{:S(2)}) copy-start(bf16[2,32,3584]{2,1,0:T(8,128)(2,1)} %param.11) | copy-start | bytes 1376260
  61.5 302.2 %all-to-all-start = ((bf16[32,112,896]{2,1,0:T(8,128)(2,1)}), bf16[32,112,896]{2,1,0:T(8,128)(2,1)}, u32[]{:S(2)}, u32[]{:S(2)}) async-start(bf16[32,112,896]{2,1,0:T(8,128)(2,1)} %stack.8), calls=%async_computation | async-start | bytes 12845056 | tf_op jit(solution)/shard_map/all_to_all | solution.py:14
  363.8 9.8 %copy-start.7 = (f32[3584]{0:T(1024)S(1)}, f32[3584]{0:T(1024)}, u32[]{:S(2)}) copy-start(f32[3584]{0:T(1024)} %param.15) | copy-start | bytes 43012
  363.8 9.8 %copy-start.8 = (f32[3584]{0:T(1024)S(1)}, f32[3584]{0:T(1024)}, u32[]{:S(2)}) copy-start(f32[3584]{0:T(1024)} %param.16) | copy-start | bytes 43012
  370.0 26.7 %all-to-all-start.2 = ((bf16[4,2,32,3584]{3,2,1,0:T(8,128)(2,1)}), bf16[4,2,32,3584]{3,2,1,0:T(8,128)(2,1)S(1)}, u32[]{:S(2)}, u32[]{:S(2)}) async-start(bf16[4,2,32,3584]{3,2,1,0:T(8,128)(2,1)} %fusion.7), calls=%async_computation.2 | async-start | bytes 3670016 | tf_op jit(solution)/shard_map/all_to_all | solution.py:69
  373.6 65.3 %all-gather.3.cloned.1.call-start = ((), (), s32[]{:S(2)}) async-start(), calls=%async_computation.7 | async-start | bytes 2293760 | tf_op jit(solution)/shard_map/all_gather | solution.py:80
  399.1 29.7 %all-to-all-start.3 = ((f32[128,2,128]{2,1,0:T(2,128)}), f32[128,2,128]{2,1,0:T(2,128)S(1)}, u32[]{:S(2)}, u32[]{:S(2)}) async-start(f32[128,2,128]{2,1,0:T(2,128)} %broadcast_in_dim.14), calls=%async_computation.3 | async-start | bytes 262144 | tf_op jit(solution)/shard_map/all_to_all | solution.py:20
  431.6 16.3 %all-to-all-start.4 = ((f32[32,2,128]{2,1,0:T(2,128)}), f32[32,2,128]{2,1,0:T(2,128)S(1)}, u32[]{:S(2)}, u32[]{:S(2)}) async-start(f32[32,2,128]{2,1,0:T(2,128)} %copy.35), calls=%async_computation.4 | async-start | bytes 65536 | tf_op jit(solution)/shard_map/all_to_all | solution.py:100
  440.9 7.0 %copy-start.9 = (f32[2]{0:T(128)S(1)}, f32[2]{0:T(128)}, u32[]{:S(2)}) copy-start(f32[2]{0:T(128)} %param.19) | copy-start | bytes 28
  440.9 7.1 %copy-start.3 = (bf16[2,128,896]{2,1,0:T(8,128)(2,1)S(1)}, bf16[2,128,896]{2,1,0:T(8,128)(2,1)}, u32[]{:S(2)}) copy-start(bf16[2,128,896]{2,1,0:T(8,128)(2,1)} %param.10) | copy-start | bytes 1376260
  449.2 16.0 %all-to-all-start.5 = ((f32[32,8,128]{2,1,0:T(8,128)}), f32[32,8,128]{2,1,0:T(8,128)S(1)}, u32[]{:S(2)}, u32[]{:S(2)}) async-start(f32[32,8,128]{2,1,0:T(8,128)} %select_maximum_fusion), calls=%async_computation.5 | async-start | bytes 262144 | tf_op jit(solution)/shard_map/all_to_all | solution.py:150
  479.7 14.8 %all-to-all-start.6 = ((f32[32,8,128]{2,1,0:T(8,128)}), f32[32,8,128]{2,1,0:T(8,128)S(1)}, u32[]{:S(2)}, u32[]{:S(2)}) async-start(f32[32,8,128]{2,1,0:T(8,128)} %broadcast_in_dim.17), calls=%async_computation.6 | async-start | bytes 262144 | tf_op jit(solution)/shard_map/all_to_all | solution.py:153
Sparse Core Ops, SparseCore 0:
  398.4 33.9 all-gather.2
